TPU v7x, 512 devices: a whole 4x4x16 slice. The times are simulated.
512 devices in a mesh: kern: 4 (over y), tile: 128 (over x, z, core).
Axes of the slice: x: 4, y: 4, z: 16, core: 2. Of those that a mesh axis runs over, the one named last changes fastest.
Arguments:
- diag_tiles: float32 [4, 128, 512, 512], P('kern', 'tile'), may hold values from -0.25 to 0.25
- left_factors: float32 [4, 128, 8, 80, 512], P('kern', 'tile'), may hold values from -0.25 to 0.25
- right_factors: float32 [4, 128, 12, 80, 512], P('kern', 'tile'), may hold values from -0.25 to 0.25
- tile_offsets: int32 [4, 128, 8], P('kern', 'tile'), may hold values from -6 to 6, as said below
- tile_ranks: int32 [4, 128, 8], P('kern', 'tile'), may hold values from 32 to 80
- mixing: float32 [64, 4, 4], replicated, may hold values from -3 to 3
- block_index: int32 [65536], P('tile'), may hold values from 0 to 63
- rhs_field: float32 [4, 65536, 128], P('kern', 'tile'), may hold values from -6 to 6
Outputs:
- product: float32 [4, 65536, 128], P('kern', 'tile')
Inputs may be any that keep to these rules, and one draw needn't show every extreme that they name: `tile_offsets`: each row's 8 offsets are distinct and nonzero.
All inputs are finite; a program needn't handle non-finite values.
Results may differ from a plain program's by a relative error of at most 0.00007.
Values sent between devices are 32-bit elements; how exact they have to be, the bound alone decides.
A program may use at most 64 MiB of HBM per device.

v0:
```python
import jax
import jax.numpy as jnp
from jax import lax
from jax.sharding import PartitionSpec as P

REACH = 6


highest = lax.Precision.HIGHEST


def shifted(value, axis, steps):
    count = lax.axis_size(axis)
    pairs = [(source, (source + steps) % count) for source in range(count)]
    return lax.ppermute(value, axis, pairs)


def deliver(coeffs):
    lower = []
    upper = []
    for stride, outbox, inbox in ((1, coeffs[:REACH][::-1], lower), (-1, coeffs[REACH:], upper)):
        for travel in range(REACH):
            outbox = shifted(outbox, "tile", stride)
            inbox.append(outbox[0])
            outbox = outbox[1:]
    return jnp.stack(lower[::-1] + upper)


def apply_kernel(diag_tile, left_tile, right_tile, offsets_row, ranks_row, column_vals):
    coeffs = jnp.einsum("sqp,pc->sqc", right_tile, column_vals, precision=highest)
    arrived = deliver(coeffs)
    slot_pick = jnp.where(offsets_row < 0, offsets_row + REACH, offsets_row + REACH - 1)
    picker = (slot_pick[:, None] == jnp.arange(2 * REACH)[None, :]).astype(jnp.float32)
    chosen = jnp.einsum("ks,sqc->kqc", picker, arrived, precision=highest)
    keeper = (jnp.arange(left_tile.shape[1])[None, :] < ranks_row[:, None]).astype(jnp.float32)
    chosen = chosen * keeper[:, :, None]
    result = jnp.dot(diag_tile, column_vals, precision=highest, preferred_element_type=jnp.float32)
    return result + jnp.einsum("kqp,kqc->pc", left_tile, chosen, precision=highest)


def local(
    diag_tiles,
    left_factors,
    right_factors,
    tile_offsets,
    tile_ranks,
    mixing,
    block_index,
    rhs_field,
):
    diag_tile = diag_tiles[0, 0]
    left_tile = left_factors[0, 0]
    right_tile = right_factors[0, 0]
    offsets_row = tile_offsets[0, 0]
    ranks_row = tile_ranks[0, 0]
    first = apply_kernel(diag_tile, left_tile, right_tile, offsets_row, ranks_row, rhs_field[0])
    own_group = lax.axis_index("kern")
    table_len = mixing.shape[0]
    grouped = lax.all_to_all(first[None], "kern", split_axis=1, concat_axis=0, tiled=True)
    part_len = grouped.shape[1]
    local_index = lax.dynamic_slice_in_dim(block_index, own_group * part_len, part_len)
    picker = (jnp.arange(table_len)[:, None] == local_index[None, :]).astype(jnp.float32)
    full_mix = jnp.einsum("nab,nl->abl", mixing, picker, precision=highest)
    blended = jnp.einsum("abl,blc->alc", full_mix, grouped, precision=highest)
    mixed = lax.all_to_all(blended, "kern", split_axis=0, concat_axis=1, tiled=True)[0]
    second = apply_kernel(diag_tile, left_tile, right_tile, offsets_row, ranks_row, mixed)
    return second[None]


def solution(mesh):
    in_specs = (
        P("kern", "tile", None, None),
        P("kern", "tile", None, None, None),
        P("kern", "tile", None, None, None),
        P("kern", "tile", None),
        P("kern", "tile", None),
        P(),
        P("tile"),
        P("kern", "tile", None),
    )
    out_specs = P("kern", "tile", None)
    return jax.shard_map(local, mesh=mesh, in_specs=in_specs, out_specs=out_specs, check_vma=False)
```

profile of v0, /device:TPU:8, one launch (start us, length us, event | category | flops | bytes accessed | tf_op | source)
XLA Modules:
  0.0 187.4 jit_solution(5393863656970466606)
XLA Ops:
  1.5 2.6 %fusion.2 = f32[12,80,128]{2,1,0:T(8,128)S(1)} fusion(f32[1,1,12,80,512]{4,3,2,1,0:T(8,128)S(1)} %copy-done, f32[1,512,128]{2,1,0:T(8,128)} %param.15), kind=kOutput, calls=%fused_computation.2 | convolution fusion | flops 754974720 | bytes 2719744 | tf_op jit(solution)/shard_map/sqp,pc->sqc/dot_general | solution.py:30
  6.2 13.0 %collective-permute-start.6 = (f32[6,80,128]{2,1,0:T(8,128)S(1)}, f32[6,80,128]{2,1,0:T(8,128)S(1)}, u32[]{:S(2)}, u32[]{:S(2)}) collective-permute-start(f32[6,80,128]{2,1,0:T(8,128)S(1)} %get-tuple-element.7), channel_id=1, source_target_pairs={{0,127},{1,0},{2,1},{3,2},{4,3},{5,4},{6,5},{7,6},{8,7},{9,8},{10,... | collective-permute-start | bytes 737288 | tf_op jit(solution)/shard_map/ppermute | solution.py:15
  19.2 1.9 %collective-permute-done = f32[6,80,128]{2,1,0:T(8,128)S(1)} collective-permute-done((f32[6,80,128]{2,1,0:T(8,128)S(1)}, f32[6,80,128]{2,1,0:T(8,128)S(1)}, u32[]{:S(2)}, u32[]{:S(2)}) %collective-permute-start) | collective-permute-done | bytes 245792 | tf_op jit(solution)/shard_map/ppermute | solution.py:15
  23.2 7.0 %collective-permute-start.7 = (f32[5,80,128]{2,1,0:T(8,128)S(1)}, f32[5,80,128]{2,1,0:T(8,128)S(1)}, u32[]{:S(2)}, u32[]{:S(2)}) collective-permute-start(f32[5,80,128]{2,1,0:T(8,128)S(1)} %slice.189), channel_id=1, source_target_pairs={{0,127},{1,0},{2,1},{3,2},{4,3},{5,4},{6,5},{7,6},{8,7},{9,8},{10,... | collective-permute-start | bytes 614408 | tf_op jit(solution)/shard_map/ppermute | solution.py:15
  33.5 8.0 %collective-permute-done.2 = f32[4,80,128]{2,1,0:T(8,128)S(1)} collective-permute-done((f32[4,80,128]{2,1,0:T(8,128)S(1)}, f32[4,80,128]{2,1,0:T(8,128)S(1)}, u32[]{:S(2)}, u32[]{:S(2)}) %collective-permute-start.2) | collective-permute-done | bytes 163872 | tf_op jit(solution)/shard_map/ppermute | solution.py:15
  41.6 1.9 %collective-permute-start.3 = (f32[3,80,128]{2,1,0:T(8,128)S(1)}, f32[3,80,128]{2,1,0:T(8,128)S(1)}, u32[]{:S(2)}, u32[]{:S(2)}) collective-permute-start(f32[3,80,128]{2,1,0:T(8,128)S(1)} %slice.179), channel_id=1, source_target_pairs={{0,1},{1,2},{2,3},{3,4},{4,5},{5,6},{6,7},{7,8},{8,9},{9,10},{10,1... | collective-permute-start | bytes 368648 | tf_op jit(solution)/shard_map/ppermute | solution.py:15
  43.5 7.0 %collective-permute-start.8 = (f32[4,80,128]{2,1,0:T(8,128)S(1)}, f32[4,80,128]{2,1,0:T(8,128)S(1)}, u32[]{:S(2)}, u32[]{:S(2)}) collective-permute-start(f32[4,80,128]{2,1,0:T(8,128)S(1)} %slice.191), channel_id=1, source_target_pairs={{0,127},{1,0},{2,1},{3,2},{4,3},{5,4},{6,5},{7,6},{8,7},{9,8},{10,... | collective-permute-start | bytes 491528 | tf_op jit(solution)/shard_map/ppermute | solution.py:15
  51.1 2.1 %collective-permute-start.4 = (f32[2,80,128]{2,1,0:T(8,128)S(1)}, f32[2,80,128]{2,1,0:T(8,128)S(1)}, u32[]{:S(2)}, u32[]{:S(2)}) collective-permute-start(f32[2,80,128]{2,1,0:T(8,128)S(1)} %slice.180), channel_id=1, source_target_pairs={{0,1},{1,2},{2,3},{3,4},{4,5},{5,6},{6,7},{7,8},{8,9},{9,10},{10,1... | collective-permute-start | bytes 245768 | tf_op jit(solution)/shard_map/ppermute | solution.py:15
  53.3 7.1 %collective-permute-start.9 = (f32[3,80,128]{2,1,0:T(8,128)S(1)}, f32[3,80,128]{2,1,0:T(8,128)S(1)}, u32[]{:S(2)}, u32[]{:S(2)}) collective-permute-start(f32[3,80,128]{2,1,0:T(8,128)S(1)} %slice.193), channel_id=1, source_target_pairs={{0,127},{1,0},{2,1},{3,2},{4,3},{5,4},{6,5},{7,6},{8,7},{9,8},{10,... | collective-permute-start | bytes 368648 | tf_op jit(solution)/shard_map/ppermute | solution.py:15
  62.9 7.1 %collective-permute-start.10 = (f32[2,80,128]{2,1,0:T(8,128)S(1)}, f32[2,80,128]{2,1,0:T(8,128)S(1)}, u32[]{:S(2)}, u32[]{:S(2)}) collective-permute-start(f32[2,80,128]{2,1,0:T(8,128)S(1)} %slice.195), channel_id=1, source_target_pairs={{0,127},{1,0},{2,1},{3,2},{4,3},{5,4},{6,5},{7,6},{8,7},{9,8},{10,... | collective-permute-start | bytes 245768 | tf_op jit(solution)/shard_map/ppermute | solution.py:15
  76.8 2.9 %collective-permute-start.11 = (f32[1,80,128]{2,1,0:T(8,128)S(1)}, f32[1,80,128]{2,1,0:T(8,128)S(1)}, u32[]{:S(2)}, u32[]{:S(2)}) collective-permute-start(f32[1,80,128]{2,1,0:T(8,128)S(1)} %get-tuple-element.11), channel_id=1, source_target_pairs={{0,127},{1,0},{2,1},{3,2},{4,3},{5,4},{6,5},{7,6},{8,7},{9,8},{10,... | collective-permute-start | bytes 122888 | tf_op jit(solution)/shard_map/ppermute | solution.py:15
  83.6 2.8 %fusion.11 = f32[512,128]{1,0:T(8,128)S(1)} fusion(f32[8,80,128]{2,0,1:T(8,128)S(1)} %convolution_multiply_fusion.1, f32[8,80,512]{2,1,0:T(8,128)S(1)} %bitcast.57), kind=kOutput, calls=%fused_computation.12 | convolution fusion | flops 503316480 | bytes 1900544 | tf_op jit(solution)/shard_map/kqp,kqc->pc/dot_general | solution.py:38
  88.1 4.9 %all-to-all-start = ((f32[1,512,128]{2,0,1:T(1,128)}), f32[1,512,128]{2,0,1:T(1,128)S(1)}, u32[]{:S(2)}, u32[]{:S(2)}) async-start(f32[1,512,128]{2,0,1:T(1,128)} %bitcast.62), calls=%async_computation | async-start | bytes 524288 | tf_op jit(solution)/shard_map/all_to_all | solution.py:59
  94.7 3.6 %all-to-all-done = f32[1,512,128]{2,0,1:T(1,128)S(1)} async-done(((f32[1,512,128]{2,0,1:T(1,128)}), f32[1,512,128]{2,0,1:T(1,128)S(1)}, u32[]{:S(2)}, u32[]{:S(2)}) %all-to-all-start) | async-done | bytes 262176 | tf_op jit(solution)/shard_map/all_to_all | solution.py:59
  98.2 2.0 %convolution_bitcast_fusion = f32[4,128,128]{2,0,1:T(4,128)S(1)} fusion(f32[4,4,128]{1,0,2:T(4,128)} %copy.30, f32[4,128,128]{2,1,0:T(8,128)S(1)} %bitcast.61), kind=kOutput, calls=%fused_computation.11 | convolution fusion | flops 3145728 | bytes 532480 | tf_op jit(solution)/shard_map/abl,blc->alc/dot_general | solution.py:64
  100.3 9.1 %all_to_all.21 = f32[4,128,128]{2,1,0:T(8,128)S(1)} all-to-all(f32[4,128,128]{2,1,0:T(8,128)S(1)} %copy.31), channel_id=1, replica_groups=mesh['kern'=4,'tile'=128] {'kern'}, dimensions={0} | all-to-all | bytes 524288 | tf_op jit(solution)/shard_map/all_to_all | solution.py:65
  115.4 7.0 %collective-permute-start.18 = (f32[6,80,128]{2,1,0:T(8,128)}, f32[6,80,128]{2,1,0:T(8,128)S(1)}, u32[]{:S(2)}, u32[]{:S(2)}) collective-permute-start(f32[6,80,128]{2,1,0:T(8,128)} %get-tuple-element.5), channel_id=1, source_target_pairs={{0,127},{1,0},{2,1},{3,2},{4,3},{5,4},{6,5},{7,6},{8,7},{9,8},{10,... | collective-permute-start | bytes 737288 | tf_op jit(solution)/shard_map/ppermute | solution.py:15
  122.4 2.1 %collective-permute-done.12 = f32[6,80,128]{2,1,0:T(8,128)S(1)} collective-permute-done((f32[6,80,128]{2,1,0:T(8,128)}, f32[6,80,128]{2,1,0:T(8,128)S(1)}, u32[]{:S(2)}, u32[]{:S(2)}) %collective-permute-start.12) | collective-permute-done | bytes 245792 | tf_op jit(solution)/shard_map/ppermute | solution.py:15
  126.6 7.0 %collective-permute-start.19 = (f32[5,80,128]{2,1,0:T(8,128)S(1)}, f32[5,80,128]{2,1,0:T(8,128)S(1)}, u32[]{:S(2)}, u32[]{:S(2)}) collective-permute-start(f32[5,80,128]{2,1,0:T(8,128)S(1)} %slice.211), channel_id=1, source_target_pairs={{0,127},{1,0},{2,1},{3,2},{4,3},{5,4},{6,5},{7,6},{8,7},{9,8},{10,... | collective-permute-start | bytes 614408 | tf_op jit(solution)/shard_map/ppermute | solution.py:15
  136.9 7.0 %collective-permute-start.20 = (f32[4,80,128]{2,1,0:T(8,128)S(1)}, f32[4,80,128]{2,1,0:T(8,128)S(1)}, u32[]{:S(2)}, u32[]{:S(2)}) collective-permute-start(f32[4,80,128]{2,1,0:T(8,128)S(1)} %slice.213), channel_id=1, source_target_pairs={{0,127},{1,0},{2,1},{3,2},{4,3},{5,4},{6,5},{7,6},{8,7},{9,8},{10,... | collective-permute-start | bytes 491528 | tf_op jit(solution)/shard_map/ppermute | solution.py:15
  146.9 7.0 %collective-permute-start.21 = (f32[3,80,128]{2,1,0:T(8,128)S(1)}, f32[3,80,128]{2,1,0:T(8,128)S(1)}, u32[]{:S(2)}, u32[]{:S(2)}) collective-permute-start(f32[3,80,128]{2,1,0:T(8,128)S(1)} %slice.215), channel_id=1, source_target_pairs={{0,127},{1,0},{2,1},{3,2},{4,3},{5,4},{6,5},{7,6},{8,7},{9,8},{10,... | collective-permute-start | bytes 368648 | tf_op jit(solution)/shard_map/ppermute | solution.py:15
  156.4 7.2 %collective-permute-done.16 = f32[2,80,128]{2,1,0:T(8,128)S(1)} collective-permute-done((f32[2,80,128]{2,1,0:T(8,128)S(1)}, f32[2,80,128]{2,1,0:T(8,128)S(1)}, u32[]{:S(2)}, u32[]{:S(2)}) %collective-permute-start.16) | collective-permute-done | bytes 81952 | tf_op jit(solution)/shard_map/ppermute | solution.py:15
  165.5 7.0 %collective-permute-start.22 = (f32[2,80,128]{2,1,0:T(8,128)S(1)}, f32[2,80,128]{2,1,0:T(8,128)S(1)}, u32[]{:S(2)}, u32[]{:S(2)}) collective-permute-start(f32[2,80,128]{2,1,0:T(8,128)S(1)} %slice.217), channel_id=1, source_target_pairs={{0,127},{1,0},{2,1},{3,2},{4,3},{5,4},{6,5},{7,6},{8,7},{9,8},{10,... | collective-permute-start | bytes 245768 | tf_op jit(solution)/shard_map/ppermute | solution.py:15
  174.5 7.0 %collective-permute-start.23 = (f32[1,80,128]{2,1,0:T(8,128)S(1)}, f32[1,80,128]{2,1,0:T(8,128)S(1)}, u32[]{:S(2)}, u32[]{:S(2)}) collective-permute-start(f32[1,80,128]{2,1,0:T(8,128)S(1)} %get-tuple-element.9), channel_id=1, source_target_pairs={{0,127},{1,0},{2,1},{3,2},{4,3},{5,4},{6,5},{7,6},{8,7},{9,8},{10,... | collective-permute-start | bytes 122888 | tf_op jit(solution)/shard_map/ppermute | solution.py:15
  (113 shorter events, 52.6 us)
Async XLA Ops:
  4.3 16.9 %collective-permute-start = (f32[6,80,128]{2,1,0:T(8,128)S(1)}, f32[6,80,128]{2,1,0:T(8,128)S(1)}, u32[]{:S(2)}, u32[]{:S(2)}) collective-permute-start(f32[6,80,128]{2,1,0:T(8,128)S(1)} %rev.6), channel_id=1, source_target_pairs={{0,1},{1,2},{2,3},{3,4},{4,5},{5,6},{6,7},{7,8},{8,9},{9,10},{10,1... | collective-permute-start | bytes 737288 | tf_op jit(solution)/shard_map/ppermute | solution.py:15
  6.2 16.9 %collective-permute-start.6 = (f32[6,80,128]{2,1,0:T(8,128)S(1)}, f32[6,80,128]{2,1,0:T(8,128)S(1)}, u32[]{:S(2)}, u32[]{:S(2)}) collective-permute-start(f32[6,80,128]{2,1,0:T(8,128)S(1)} %get-tuple-element.7), channel_id=1, source_target_pairs={{0,127},{1,0},{2,1},{3,2},{4,3},{5,4},{6,5},{7,6},{8,7},{9,8},{10,... | collective-permute-start | bytes 737288 | tf_op jit(solution)/shard_map/ppermute | solution.py:15
  21.2 10.4 %collective-permute-start.1 = (f32[5,80,128]{2,1,0:T(8,128)S(1)}, f32[5,80,128]{2,1,0:T(8,128)S(1)}, u32[]{:S(2)}, u32[]{:S(2)}) collective-permute-start(f32[5,80,128]{2,1,0:T(8,128)S(1)} %slice.177), channel_id=1, source_target_pairs={{0,1},{1,2},{2,3},{3,4},{4,5},{5,6},{6,7},{7,8},{8,9},{9,10},{10,1... | collective-permute-start | bytes 614408 | tf_op jit(solution)/shard_map/ppermute | solution.py:15
  23.2 20.3 %collective-permute-start.7 = (f32[5,80,128]{2,1,0:T(8,128)S(1)}, f32[5,80,128]{2,1,0:T(8,128)S(1)}, u32[]{:S(2)}, u32[]{:S(2)}) collective-permute-start(f32[5,80,128]{2,1,0:T(8,128)S(1)} %slice.189), channel_id=1, source_target_pairs={{0,127},{1,0},{2,1},{3,2},{4,3},{5,4},{6,5},{7,6},{8,7},{9,8},{10,... | collective-permute-start | bytes 614408 | tf_op jit(solution)/shard_map/ppermute | solution.py:15
  31.6 10.0 %collective-permute-start.2 = (f32[4,80,128]{2,1,0:T(8,128)S(1)}, f32[4,80,128]{2,1,0:T(8,128)S(1)}, u32[]{:S(2)}, u32[]{:S(2)}) collective-permute-start(f32[4,80,128]{2,1,0:T(8,128)S(1)} %slice.178), channel_id=1, source_target_pairs={{0,1},{1,2},{2,3},{3,4},{4,5},{5,6},{6,7},{7,8},{8,9},{9,10},{10,1... | collective-permute-start | bytes 491528 | tf_op jit(solution)/shard_map/ppermute | solution.py:15
  41.6 9.5 %collective-permute-start.3 = (f32[3,80,128]{2,1,0:T(8,128)S(1)}, f32[3,80,128]{2,1,0:T(8,128)S(1)}, u32[]{:S(2)}, u32[]{:S(2)}) collective-permute-start(f32[3,80,128]{2,1,0:T(8,128)S(1)} %slice.179), channel_id=1, source_target_pairs={{0,1},{1,2},{2,3},{3,4},{4,5},{5,6},{6,7},{7,8},{8,9},{9,10},{10,1... | collective-permute-start | bytes 368648 | tf_op jit(solution)/shard_map/ppermute | solution.py:15
  43.5 9.8 %collective-permute-start.8 = (f32[4,80,128]{2,1,0:T(8,128)S(1)}, f32[4,80,128]{2,1,0:T(8,128)S(1)}, u32[]{:S(2)}, u32[]{:S(2)}) collective-permute-start(f32[4,80,128]{2,1,0:T(8,128)S(1)} %slice.191), channel_id=1, source_target_pairs={{0,127},{1,0},{2,1},{3,2},{4,3},{5,4},{6,5},{7,6},{8,7},{9,8},{10,... | collective-permute-start | bytes 491528 | tf_op jit(solution)/shard_map/ppermute | solution.py:15
  51.1 9.4 %collective-permute-start.4 = (f32[2,80,128]{2,1,0:T(8,128)S(1)}, f32[2,80,128]{2,1,0:T(8,128)S(1)}, u32[]{:S(2)}, u32[]{:S(2)}) collective-permute-start(f32[2,80,128]{2,1,0:T(8,128)S(1)} %slice.180), channel_id=1, source_target_pairs={{0,1},{1,2},{2,3},{3,4},{4,5},{5,6},{6,7},{7,8},{8,9},{9,10},{10,1... | collective-permute-start | bytes 245768 | tf_op jit(solution)/shard_map/ppermute | solution.py:15
  53.3 9.6 %collective-permute-start.9 = (f32[3,80,128]{2,1,0:T(8,128)S(1)}, f32[3,80,128]{2,1,0:T(8,128)S(1)}, u32[]{:S(2)}, u32[]{:S(2)}) collective-permute-start(f32[3,80,128]{2,1,0:T(8,128)S(1)} %slice.193), channel_id=1, source_target_pairs={{0,127},{1,0},{2,1},{3,2},{4,3},{5,4},{6,5},{7,6},{8,7},{9,8},{10,... | collective-permute-start | bytes 368648 | tf_op jit(solution)/shard_map/ppermute | solution.py:15
  60.5 9.5 %collective-permute-start.5 = (f32[1,80,128]{2,1,0:T(8,128)S(1)}, f32[1,80,128]{2,1,0:T(8,128)S(1)}, u32[]{:S(2)}, u32[]{:S(2)}) collective-permute-start(f32[1,80,128]{2,1,0:T(8,128)S(1)} %slice.181), channel_id=1, source_target_pairs={{0,1},{1,2},{2,3},{3,4},{4,5},{5,6},{6,7},{7,8},{8,9},{9,10},{10,1... | collective-permute-start | bytes 122888 | tf_op jit(solution)/shard_map/ppermute | solution.py:15
  62.9 13.3 %collective-permute-start.10 = (f32[2,80,128]{2,1,0:T(8,128)S(1)}, f32[2,80,128]{2,1,0:T(8,128)S(1)}, u32[]{:S(2)}, u32[]{:S(2)}) collective-permute-start(f32[2,80,128]{2,1,0:T(8,128)S(1)} %slice.195), channel_id=1, source_target_pairs={{0,127},{1,0},{2,1},{3,2},{4,3},{5,4},{6,5},{7,6},{8,7},{9,8},{10,... | collective-permute-start | bytes 245768 | tf_op jit(solution)/shard_map/ppermute | solution.py:15
  88.1 10.1 %all-to-all-start = ((f32[1,512,128]{2,0,1:T(1,128)}), f32[1,512,128]{2,0,1:T(1,128)S(1)}, u32[]{:S(2)}, u32[]{:S(2)}) async-start(f32[1,512,128]{2,0,1:T(1,128)} %bitcast.62), calls=%async_computation | async-start | bytes 524288 | tf_op jit(solution)/shard_map/all_to_all | solution.py:59
  113.5 11.0 %collective-permute-start.12 = (f32[6,80,128]{2,1,0:T(8,128)}, f32[6,80,128]{2,1,0:T(8,128)S(1)}, u32[]{:S(2)}, u32[]{:S(2)}) collective-permute-start(f32[6,80,128]{2,1,0:T(8,128)} %rev.7), channel_id=1, source_target_pairs={{0,1},{1,2},{2,3},{3,4},{4,5},{5,6},{6,7},{7,8},{8,9},{9,10},{10,1... | collective-permute-start | bytes 737288 | tf_op jit(solution)/shard_map/ppermute | solution.py:15
  115.4 11.1 %collective-permute-start.18 = (f32[6,80,128]{2,1,0:T(8,128)}, f32[6,80,128]{2,1,0:T(8,128)S(1)}, u32[]{:S(2)}, u32[]{:S(2)}) collective-permute-start(f32[6,80,128]{2,1,0:T(8,128)} %get-tuple-element.5), channel_id=1, source_target_pairs={{0,127},{1,0},{2,1},{3,2},{4,3},{5,4},{6,5},{7,6},{8,7},{9,8},{10,... | collective-permute-start | bytes 737288 | tf_op jit(solution)/shard_map/ppermute | solution.py:15
  124.6 10.4 %collective-permute-start.13 = (f32[5,80,128]{2,1,0:T(8,128)S(1)}, f32[5,80,128]{2,1,0:T(8,128)S(1)}, u32[]{:S(2)}, u32[]{:S(2)}) collective-permute-start(f32[5,80,128]{2,1,0:T(8,128)S(1)} %slice.199), channel_id=1, source_target_pairs={{0,1},{1,2},{2,3},{3,4},{4,5},{5,6},{6,7},{7,8},{8,9},{9,10},{10,1... | collective-permute-start | bytes 614408 | tf_op jit(solution)/shard_map/ppermute | solution.py:15
  126.6 10.4 %collective-permute-start.19 = (f32[5,80,128]{2,1,0:T(8,128)S(1)}, f32[5,80,128]{2,1,0:T(8,128)S(1)}, u32[]{:S(2)}, u32[]{:S(2)}) collective-permute-start(f32[5,80,128]{2,1,0:T(8,128)S(1)} %slice.211), channel_id=1, source_target_pairs={{0,127},{1,0},{2,1},{3,2},{4,3},{5,4},{6,5},{7,6},{8,7},{9,8},{10,... | collective-permute-start | bytes 614408 | tf_op jit(solution)/shard_map/ppermute | solution.py:15
  135.0 10.0 %collective-permute-start.14 = (f32[4,80,128]{2,1,0:T(8,128)S(1)}, f32[4,80,128]{2,1,0:T(8,128)S(1)}, u32[]{:S(2)}, u32[]{:S(2)}) collective-permute-start(f32[4,80,128]{2,1,0:T(8,128)S(1)} %slice.200), channel_id=1, source_target_pairs={{0,1},{1,2},{2,3},{3,4},{4,5},{5,6},{6,7},{7,8},{8,9},{9,10},{10,1... | collective-permute-start | bytes 491528 | tf_op jit(solution)/shard_map/ppermute | solution.py:15
  136.9 9.9 %collective-permute-start.20 = (f32[4,80,128]{2,1,0:T(8,128)S(1)}, f32[4,80,128]{2,1,0:T(8,128)S(1)}, u32[]{:S(2)}, u32[]{:S(2)}) collective-permute-start(f32[4,80,128]{2,1,0:T(8,128)S(1)} %slice.213), channel_id=1, source_target_pairs={{0,127},{1,0},{2,1},{3,2},{4,3},{5,4},{6,5},{7,6},{8,7},{9,8},{10,... | collective-permute-start | bytes 491528 | tf_op jit(solution)/shard_map/ppermute | solution.py:15
  145.0 9.5 %collective-permute-start.15 = (f32[3,80,128]{2,1,0:T(8,128)S(1)}, f32[3,80,128]{2,1,0:T(8,128)S(1)}, u32[]{:S(2)}, u32[]{:S(2)}) collective-permute-start(f32[3,80,128]{2,1,0:T(8,128)S(1)} %slice.201), channel_id=1, source_target_pairs={{0,1},{1,2},{2,3},{3,4},{4,5},{5,6},{6,7},{7,8},{8,9},{9,10},{10,1... | collective-permute-start | bytes 368648 | tf_op jit(solution)/shard_map/ppermute | solution.py:15
  146.9 18.6 %collective-permute-start.21 = (f32[3,80,128]{2,1,0:T(8,128)S(1)}, f32[3,80,128]{2,1,0:T(8,128)S(1)}, u32[]{:S(2)}, u32[]{:S(2)}) collective-permute-start(f32[3,80,128]{2,1,0:T(8,128)S(1)} %slice.215), channel_id=1, source_target_pairs={{0,127},{1,0},{2,1},{3,2},{4,3},{5,4},{6,5},{7,6},{8,7},{9,8},{10,... | collective-permute-start | bytes 368648 | tf_op jit(solution)/shard_map/ppermute | solution.py:15
  154.5 9.1 %collective-permute-start.16 = (f32[2,80,128]{2,1,0:T(8,128)S(1)}, f32[2,80,128]{2,1,0:T(8,128)S(1)}, u32[]{:S(2)}, u32[]{:S(2)}) collective-permute-start(f32[2,80,128]{2,1,0:T(8,128)S(1)} %slice.202), channel_id=1, source_target_pairs={{0,1},{1,2},{2,3},{3,4},{4,5},{5,6},{6,7},{7,8},{8,9},{9,10},{10,1... | collective-permute-start | bytes 245768 | tf_op jit(solution)/shard_map/ppermute | solution.py:15
  163.6 8.9 %collective-permute-start.17 = (f32[1,80,128]{2,1,0:T(8,128)S(1)}, f32[1,80,128]{2,1,0:T(8,128)S(1)}, u32[]{:S(2)}, u32[]{:S(2)}) collective-permute-start(f32[1,80,128]{2,1,0:T(8,128)S(1)} %slice.203), channel_id=1, source_target_pairs={{0,1},{1,2},{2,3},{3,4},{4,5},{5,6},{6,7},{7,8},{8,9},{9,10},{10,1... | collective-permute-start | bytes 122888 | tf_op jit(solution)/shard_map/ppermute | solution.py:15
  165.5 9.0 %collective-permute-start.22 = (f32[2,80,128]{2,1,0:T(8,128)S(1)}, f32[2,80,128]{2,1,0:T(8,128)S(1)}, u32[]{:S(2)}, u32[]{:S(2)}) collective-permute-start(f32[2,80,128]{2,1,0:T(8,128)S(1)} %slice.217), channel_id=1, source_target_pairs={{0,127},{1,0},{2,1},{3,2},{4,3},{5,4},{6,5},{7,6},{8,7},{9,8},{10,... | collective-permute-start | bytes 245768 | tf_op jit(solution)/shard_map/ppermute | solution.py:15
  174.5 8.7 %collective-permute-start.23 = (f32[1,80,128]{2,1,0:T(8,128)S(1)}, f32[1,80,128]{2,1,0:T(8,128)S(1)}, u32[]{:S(2)}, u32[]{:S(2)}) collective-permute-start(f32[1,80,128]{2,1,0:T(8,128)S(1)} %get-tuple-element.9), channel_id=1, source_target_pairs={{0,127},{1,0},{2,1},{3,2},{4,3},{5,4},{6,5},{7,6},{8,7},{9,8},{10,... | collective-permute-start | bytes 122888 | tf_op jit(solution)/shard_map/ppermute | solution.py:15
  (13 other events, 314.7 us)
where the time goes:
time: 189 us; the launch traced here: 187 us
  starting transfers between devices  114 us (60%)
  waiting for transfers between devices  32.4 us (17%)
  matrix products  16.5 us (9%)
  local copies, waits for them, and re-layouts  14.8 us (8%)
  blocking collectives  9.07 us (5%)
    ppermute x24, starting transfers between devices, shifted(): return lax.ppermute(value, axis, pairs)  109 us
    ppermute x24, waiting for transfers between devices, shifted(): return lax.ppermute(value, axis, pairs)  28.8 us
    all_to_all x1, blocking collectives, local(): lax.all_to_all(blended, 'kern', split_axis=0, concat_axis=1, tiled=True)[0]  9.07 us
    unnamed x44, local copies, waits for them, and re-layouts  7.82 us
    all_to_all x1, starting transfers between devices, local(): lax.all_to_all(first[None], 'kern', split_axis=1, concat_axis=0, tiled=True)  4.91 us
    dot_general x2, matrix products, apply_kernel(): jnp.einsum('kqp,kqc->pc', left_tile, chosen, precision=highest)  4.37 us
    dot_general x2, matrix products, apply_kernel(): jnp.einsum('sqp,pc->sqc', right_tile, column_vals, precision=highest)  4.33 us
  transfers between devices with their start and end apart: 25, of which 15 were waited for; matrix products, arithmetic and copies ran while one was open for 5% of the time, Pallas kernels for 0%

commit v1 on v0

v1 whole, which is shorter than its diff:
```python
import functools

import jax
import jax.numpy as jnp
from jax import lax
from jax.experimental import pallas as pl
from jax.experimental.pallas import tpu as pltpu
from jax.sharding import PartitionSpec as P

MESH = pl.DeviceIdType.MESH
REACH = 6
SLOTS = 2 * REACH
ORDER = tuple(slot for far in range(REACH, 0, -1) for slot in (REACH - far, REACH + far - 1))
GROUP = 3
GROUPS = SLOTS // GROUP


def offset_of(slot):
    return slot - REACH if slot < REACH else slot - REACH + 1


def split(value):
    high = value.astype(jnp.bfloat16)
    return high, (value - high.astype(jnp.float32)).astype(jnp.bfloat16)


def dot(a, b):
    return jnp.dot(a, b, preferred_element_type=jnp.float32)


def product(high, low, pair):
    width = pair.shape[1] // 2
    wide = dot(high, pair)
    return wide[:, :width] + wide[:, width:] + dot(low, pair[:, :width])


def kernel(
    tiles,
    kerns,
    diag_hbm,
    left_hbm,
    right_hbm,
    offsets_hbm,
    ranks_hbm,
    mixing_hbm,
    index_hbm,
    rhs_hbm,
    out_ref,
    column,
    diag_f32,
    left_f32,
    right_f32,
    offsets,
    ranks,
    mixing,
    index,
    diag_hi,
    diag_lo,
    right_hi,
    right_lo,
    left_hi,
    left_lo,
    pair,
    arrived_pair,
    coeffs,
    arrived,
    total,
    blend,
    gathered,
    mixed_out,
    second,
    load_sem,
    right_sem,
    send_sem,
    recv_sem,
    field_send,
    field_recv,
):
    me = lax.axis_index("tile")
    group = lax.axis_index("kern")
    rows, cols = column.shape
    rank_max = right_f32.shape[1]
    depth = arrived.shape[2]
    part = rows // kerns

    def tile_at(offset):
        return (group, lax.rem(me + offset + tiles, tiles))

    def kern_at(ahead):
        return (lax.rem(group + ahead, kerns), me)

    def part_rows(ahead):
        return pl.ds(pl.multiple_of(lax.rem(group + ahead, kerns) * part, part), part)

    barrier = pltpu.get_barrier_semaphore()
    for slot in ORDER:
        pl.semaphore_signal(barrier, inc=1, device_id=tile_at(offset_of(slot)), device_id_type=MESH)
    for ahead in range(1, kerns):
        pl.semaphore_signal(barrier, inc=1, device_id=kern_at(ahead), device_id_type=MESH)

    load_rhs = pltpu.make_async_copy(rhs_hbm.at[0], column, load_sem.at[0])
    load_rhs.start()
    load_right = []
    for place, slot in enumerate(ORDER):
        copy = pltpu.make_async_copy(right_hbm.at[0, 0, slot], right_f32.at[place], right_sem.at[place])
        copy.start()
        load_right.append(copy)
    load_left = pltpu.make_async_copy(left_hbm.at[0, 0], left_f32, load_sem.at[1])
    load_diag = pltpu.make_async_copy(diag_hbm.at[0, 0], diag_f32, load_sem.at[2])
    load_offsets = pltpu.make_async_copy(offsets_hbm, offsets, load_sem.at[3])
    load_ranks = pltpu.make_async_copy(ranks_hbm, ranks, load_sem.at[4])
    load_mixing = pltpu.make_async_copy(mixing_hbm, mixing, load_sem.at[5])
    load_index = pltpu.make_async_copy(index_hbm, index, load_sem.at[6])
    for copy in (load_offsets, load_ranks, load_left, load_diag, load_mixing, load_index):
        copy.start()

    def send_coeffs(turn, place):
        copy = pltpu.make_async_remote_copy(
            src_ref=coeffs.at[turn, place],
            dst_ref=arrived.at[turn, place // GROUP, pl.ds(place % GROUP * rank_max, rank_max)],
            send_sem=send_sem.at[turn, place],
            recv_sem=recv_sem.at[turn, place],
            device_id=tile_at(-offset_of(ORDER[place])),
            device_id_type=MESH,
        )
        copy.start()
        return copy

    def spread(turn, before_first):
        copies = []
        for place in range(SLOTS):
            if turn == 0:
                load_right[place].wait()
                high, low = split(right_f32[place])
                right_hi[place] = high
                right_lo[place] = low
            coeffs[turn, place] = product(right_hi[place], right_lo[place], pair[...])
            if place == 0:
                before_first()
            else:
                copies.append(send_coeffs(turn, place - 1))
        copies.append(send_coeffs(turn, SLOTS - 1))
        return copies

    def set_pair(target, value):
        high, low = split(value)
        target[:, :cols] = high
        target[:, cols:] = low

    def diag_part(ref):
        def body(step, carry):
            at = pl.ds(pl.multiple_of(step * part, part), part)
            ref[at] = product(diag_hi[at], diag_lo[at], pair[...])
            return carry

        lax.fori_loop(0, kerns, body, 0)

    def add_group(turn, which, at, source, ref):
        lanes = pl.ds(which * depth, depth)
        ref[at] = source[at] + product(left_hi[at, lanes], left_lo[at, lanes], arrived_pair[...])

    load_rhs.wait()
    set_pair(pair, column[...])
    first_sends = spread(0, lambda: pl.semaphore_wait(barrier, SLOTS + kerns - 1))

    load_diag.wait()

    def split_diag(step, carry):
        at = pl.ds(pl.multiple_of(step * part, part), part)
        high, low = split(diag_f32[at])
        diag_hi[at] = high
        diag_lo[at] = low
        return carry

    lax.fori_loop(0, kerns, split_diag, 0)
    diag_part(total)

    load_offsets.wait()
    load_ranks.wait()
    load_left.wait()
    pad = depth - GROUP * rank_max
    for turn in range(2):
        for which in range(GROUPS):
            arrived[turn, which, pl.ds(GROUP * rank_max, pad)] = jnp.zeros((pad, cols), jnp.float32)
    for which in range(GROUPS):
        stack = []
        for place in range(which * GROUP, which * GROUP + GROUP):
            source = jnp.int32(0)
            rank = jnp.int32(0)
            for k in range(left_f32.shape[0]):
                here = offsets[0, 0, k] == offset_of(ORDER[place])
                source = jnp.where(here, k, source)
                rank = jnp.where(here, ranks[0, 0, k], rank)
            factor = left_f32[source]
            keep = lax.broadcasted_iota(jnp.int32, factor.shape, 0) < rank
            stack.append(jnp.where(keep, factor, 0.0))
        stack.append(jnp.zeros((pad, rows), jnp.float32))
        high, low = split(jnp.transpose(jnp.concatenate(stack, axis=0)))
        left_hi[:, which * depth : which * depth + depth] = high
        left_lo[:, which * depth : which * depth + depth] = low

    load_mixing.wait()
    load_index.wait()
    table_len = mixing.shape[2]
    own_index = index[pl.ds(group, 1), :]
    picker = lax.broadcasted_iota(jnp.int32, (table_len, part), 0) == own_index
    picker = jnp.transpose(picker.astype(jnp.float32))
    for a in range(kerns):
        for b in range(kerns):
            entry = jnp.broadcast_to(mixing[a, b : b + 1], (cols, table_len))
            blend[a, b] = lax.dot_general(
                picker,
                entry,
                (((1,), (1,)), ((), ())),
                precision=lax.Precision.HIGHEST,
                preferred_element_type=jnp.float32,
            )

    def collect(turn, copies, target, after):
        for which in range(GROUPS):
            for place in range(which * GROUP, which * GROUP + GROUP):
                copies[place].wait_recv()
            set_pair(arrived_pair, arrived[turn, which])
            last = which == GROUPS - 1
            for step, ahead in enumerate(turns):
                add_group(turn, which, part_rows(ahead), total, target if last else total)
                if last:
                    after(step)

    field_copies = []
    turns = tuple(sorted(range(1, kerns), key=lambda ahead: -min(ahead, kerns - ahead))) + (0,)

    def send_first(turn):
        if turn == 0:
            return
        ahead = turns[turn - 1]
        copy = pltpu.make_async_remote_copy(
            src_ref=total.at[part_rows(ahead)],
            dst_ref=gathered.at[kerns - ahead],
            send_sem=field_send.at[0, ahead],
            recv_sem=field_recv.at[0, kerns - ahead],
            device_id=kern_at(ahead),
            device_id_type=MESH,
        )
        copy.start()
        field_copies.append(copy)

    collect(0, first_sends, total, send_first)
    for copy in field_copies:
        copy.wait_recv()

    mixed_copies = []

    def send_mixed(ahead):
        copy = pltpu.make_async_remote_copy(
            src_ref=mixed_out.at[ahead],
            dst_ref=second.at[part_rows(0)],
            send_sem=field_send.at[1, ahead],
            recv_sem=field_recv.at[1, kerns - ahead],
            device_id=kern_at(ahead),
            device_id_type=MESH,
        )
        copy.start()
        mixed_copies.append(copy)

    for step, ahead in enumerate(turns):
        to = lax.rem(group + ahead, kerns)
        value = blend[to, group] * total[part_rows(0)]
        for other in range(1, kerns):
            value += blend[to, lax.rem(group + other, kerns)] * gathered[other]
        if ahead == 0:
            second[part_rows(0)] = value
        else:
            mixed_out[ahead] = value
        if step:
            send_mixed(turns[step - 1])
    for copy in field_copies:
        copy.wait_send()
    for copy in mixed_copies:
        copy.wait_recv()

    set_pair(pair, second[...])
    second_sends = spread(1, lambda: None)
    diag_part(total)
    collect(1, second_sends, out_ref, lambda step: None)
    for copy in first_sends + mixed_copies + second_sends:
        copy.wait_send()


def local(tiles, kerns, *args):
    diag, left, right, offsets, ranks, mixing, index, rhs = args
    rows, cols = rhs.shape[1:]
    count, rank_max = left.shape[2:4]
    index = index.reshape(kerns, rows // kerns)
    mixing = mixing.transpose(1, 2, 0)
    depth = -(-GROUP * rank_max // 128) * 128
    f32, bf16 = jnp.float32, jnp.bfloat16
    vmem = pltpu.VMEM
    return pl.pallas_call(
        functools.partial(kernel, tiles, kerns),
        out_shape=jax.ShapeDtypeStruct((rows, cols), f32),
        in_specs=[pl.BlockSpec(memory_space=pl.ANY)] * 8,
        out_specs=pl.BlockSpec(memory_space=pltpu.VMEM),
        scratch_shapes=[
            vmem((rows, cols), f32),
            vmem((rows, rows), f32),
            vmem((count, rank_max, rows), f32),
            vmem((SLOTS, rank_max, rows), f32),
            pltpu.SMEM(offsets.shape, jnp.int32),
            pltpu.SMEM(ranks.shape, jnp.int32),
            vmem(mixing.shape, f32),
            vmem(index.shape, jnp.int32),
            vmem((rows, rows), bf16),
            vmem((rows, rows), bf16),
            vmem((SLOTS, rank_max, rows), bf16),
            vmem((SLOTS, rank_max, rows), bf16),
            vmem((rows, GROUPS * depth), bf16),
            vmem((rows, GROUPS * depth), bf16),
            vmem((rows, 2 * cols), bf16),
            vmem((depth, 2 * cols), bf16),
            vmem((2, SLOTS, rank_max, cols), f32),
            vmem((2, GROUPS, depth, cols), f32),
            vmem((rows, cols), f32),
            vmem((kerns, kerns, rows // kerns, cols), f32),
            vmem((kerns, rows // kerns, cols), f32),
            vmem((kerns, rows // kerns, cols), f32),
            vmem((rows, cols), f32),
            pltpu.SemaphoreType.DMA((7,)),
            pltpu.SemaphoreType.DMA((SLOTS,)),
            pltpu.SemaphoreType.DMA((2, SLOTS)),
            pltpu.SemaphoreType.DMA((2, SLOTS)),
            pltpu.SemaphoreType.DMA((2, kerns)),
            pltpu.SemaphoreType.DMA((2, kerns)),
        ],
        compiler_params=pltpu.CompilerParams(collective_id=0, has_side_effects=True),
    )(diag, left, right, offsets, ranks, mixing, index, rhs)[None]


def solution(mesh):
    in_specs = (
        P("kern", "tile", None, None),
        P("kern", "tile", None, None, None),
        P("kern", "tile", None, None, None),
        P("kern", "tile", None),
        P("kern", "tile", None),
        P(),
        P("tile"),
        P("kern", "tile", None),
    )
    out_specs = P("kern", "tile", None)
    step = functools.partial(local, mesh.shape["tile"], mesh.shape["kern"])
    return jax.shard_map(step, mesh=mesh, in_specs=in_specs, out_specs=out_specs, check_vma=False)
```

time: 189 us -> 53.7 us (0.28)
  the two profiles are of different devices: /device:TPU:8 before, /device:TPU:1 now
where the time goes in v1:
time: 53.7 us; the launch traced here: 52.9 us
  Pallas kernels  51.2 us (95%)
  local copies, waits for them, and re-layouts  1.67 us (3%)
    pallas_call x1, Pallas kernels, local(): pl.pallas_call(functools.partial(kernel, tiles, kerns), out_shape=jax.Sha...  51.2 us
    unnamed x1, local copies, waits for them, and re-layouts  1.67 us

profile of v1, /device:TPU:1, one launch (start us, length us, event | category | flops | bytes accessed | tf_op | source)
XLA Modules:
  0.0 52.9 jit_solution(266829853153763639)
XLA Ops:
  0.0 51.2 %shard_map.82 = f32[512,128]{1,0:T(8,128)} custom-call(f32[1,1,512,512]{3,2,1,0:T(8,128)} %diag_hbm.1, f32[1,1,8,80,512]{4,3,2,1,0:T(8,128)} %left_hbm.1, f32[1,1,12,80,512]{4,3,2,1,0:T(8,128)} %right_hbm.1, s32[1,1,8]{2,1,0:T(1,128)} %offsets_hbm.1, s32[1,1,8]{2,1,0:T(1,128)} %ranks_hbm.1, f32[4,4,64]{2,1,0:T(4,128)} %bitcast.4, s32[4,128]{1,0:T(4,128)} %bitcast.5, ...), custom_call_target="tpu_custom_call" | custom-call | tf_op jit(solution)/shard_map/pallas_call | solution.py:299
  51.2 1.7 %copy.10 = f32[1,512,128]{2,1,0:T(8,128)} copy(f32[1,512,128]{2,1,0:T(8,128)} %bitcast.3) | data formatting | bytes 524288

commit v2 on v0

v2 whole, which is shorter than its diff:
```python
import functools

import jax
import jax.numpy as jnp
from jax import lax
from jax.experimental import pallas as pl
from jax.experimental.pallas import tpu as pltpu
from jax.sharding import PartitionSpec as P

MESH = pl.DeviceIdType.MESH
REACH = 6
SLOTS = 2 * REACH
ORDER = tuple(slot for far in range(REACH, 0, -1) for slot in (REACH - far, REACH + far - 1))
BLOCKS = ((0, 2), (2, 6), (6, 12))
HALVES = 2


def offset_of(slot):
    return slot - REACH if slot < REACH else slot - REACH + 1


def left_lanes(value):
    return lax.broadcasted_iota(jnp.int32, value.shape, 1) < value.shape[1] // 2


def swapped(value):
    return pltpu.roll(value, value.shape[1] // 2, 1)


def parts(value):
    high = value.astype(jnp.bfloat16)
    return high, (value - high.astype(jnp.float32)).astype(jnp.bfloat16)


def pairs(packed):
    left = left_lanes(packed)
    high = packed.astype(jnp.bfloat16).astype(jnp.float32)
    low = packed - high
    upper = jnp.where(left, high, swapped(low))
    lower = jnp.where(left, swapped(high), low)
    return upper.astype(jnp.bfloat16), lower.astype(jnp.bfloat16)


def doubled(paired):
    return paired + swapped(paired)


def packed(value):
    rows = value.shape[0] // 2
    upper = value[:rows]
    return jnp.where(left_lanes(upper), upper, value[rows:])


def dot(a, b):
    return jnp.dot(a, b, preferred_element_type=jnp.float32)


def kernel(
    tiles,
    kerns,
    diag_hbm,
    left_hbm,
    right_hbm,
    offsets_hbm,
    ranks_hbm,
    mixing_hbm,
    index_hbm,
    rhs_hbm,
    out_ref,
    column,
    diag_f32,
    left_f32,
    right_f32,
    offsets,
    ranks,
    mixing,
    index,
    diag,
    right,
    left,
    pair,
    arrived_pair,
    coeffs,
    arrived_00,
    arrived_01,
    arrived_10,
    arrived_11,
    total,
    blend,
    fields,
    gathered,
    mixed_out,
    second,
    load_sem,
    right_sem,
    send_sem,
    recv_sem,
    field_send,
    field_recv,
):
    arrived = ((arrived_00, arrived_01), (arrived_10, arrived_11))
    me = lax.axis_index("tile")
    group = lax.axis_index("kern")
    rows, cols = column.shape
    count, rank_max = left_f32.shape[:2]
    half_rank = rank_max // 2
    depth = count * half_rank
    part = rows // kerns

    def tile_at(offset):
        return (group, lax.rem(me + offset + tiles, tiles))

    def kern_of(ahead):
        return lax.rem(group + ahead, kerns)

    def lanes(half):
        return pl.ds(half * cols, cols)

    barrier = pltpu.get_barrier_semaphore()
    for slot in ORDER:
        pl.semaphore_signal(barrier, inc=1, device_id=tile_at(offset_of(slot)), device_id_type=MESH)
    for ahead in range(1, kerns):
        pl.semaphore_signal(barrier, inc=1, device_id=(kern_of(ahead), me), device_id_type=MESH)

    load_rhs = pltpu.make_async_copy(rhs_hbm.at[0], column, load_sem.at[0])
    load_rhs.start()
    load_right = []
    for place, slot in enumerate(ORDER):
        copy = pltpu.make_async_copy(right_hbm.at[0, 0, slot], right_f32.at[place], right_sem.at[place])
        copy.start()
        load_right.append(copy)
    load_diag = pltpu.make_async_copy(diag_hbm.at[0, 0], diag_f32, load_sem.at[1])
    load_left = pltpu.make_async_copy(left_hbm.at[0, 0], left_f32, load_sem.at[2])
    load_offsets = pltpu.make_async_copy(offsets_hbm, offsets, load_sem.at[3])
    load_ranks = pltpu.make_async_copy(ranks_hbm, ranks, load_sem.at[4])
    load_mixing = pltpu.make_async_copy(mixing_hbm, mixing, load_sem.at[5])
    load_index = pltpu.make_async_copy(index_hbm, index, load_sem.at[6])
    for copy in (load_diag, load_offsets, load_ranks, load_left, load_mixing, load_index):
        copy.start()

    def send_coeffs(turn, half, place):
        copy = pltpu.make_async_remote_copy(
            src_ref=coeffs.at[turn, half, place],
            dst_ref=arrived[turn][half].at[place],
            send_sem=send_sem.at[turn, half, place],
            recv_sem=recv_sem.at[turn, half, place],
            device_id=tile_at(-offset_of(ORDER[place])),
            device_id_type=MESH,
        )
        copy.start()
        return copy

    def set_pair(at, half, value):
        pair[pl.ds(at, value.shape[0]), lanes(half)] = value
        pair[pl.ds(rows + at, value.shape[0]), lanes(half)] = value

    def keep_coeffs(turn, half, first, result):
        for place in range(first, first + result.shape[0] // rank_max):
            at = (place - first) * rank_max
            coeffs[turn, half, place] = packed(doubled(result[at : at + rank_max]))

    load_rhs.wait()
    for half, value in enumerate(pairs(column[...])):
        set_pair(0, half, value)
    sends = {(0, 0): [], (0, 1): [], (1, 0): [], (1, 1): []}
    for first, end in BLOCKS:
        for place in range(first, end):
            load_right[place].wait()
            high, low = parts(right_f32[place])
            at = pl.ds(place * rank_max, rank_max)
            right[at, pl.ds(0, rows)] = high
            right[at, pl.ds(rows, rows)] = low
        result = dot(right[pl.ds(first * rank_max, (end - first) * rank_max)], pair[...])
        for half in range(HALVES):
            keep_coeffs(0, half, first, result[:, half * cols : half * cols + cols])
        if first == 0:
            pl.semaphore_wait(barrier, SLOTS + kerns - 1)
        for place in range(first, end):
            sends[0, 0].append(send_coeffs(0, 0, place))

    def diag_part():
        def body(step, carry):
            at = pl.ds(pl.multiple_of(step * 2 * part, 2 * part), 2 * part)
            result = dot(diag[at], pair[...])
            for half in range(HALVES):
                total[half, at] = result[:, half * cols : half * cols + cols]
            return carry

        lax.fori_loop(0, kerns // 2, body, 0)

    load_diag.wait()
    for step in range(kerns):
        at = pl.ds(step * part, part)
        high, low = parts(diag_f32[at])
        diag[at, pl.ds(0, rows)] = high
        diag[at, pl.ds(rows, rows)] = low
    diag_part()

    load_offsets.wait()
    load_ranks.wait()
    load_left.wait()
    places = []
    upper = []
    lower = []
    for k in range(count):
        offset = offsets[0, 0, k]
        place = 2 * (REACH - jnp.abs(offset)) + jnp.where(offset > 0, 1, 0)
        places.append(jnp.clip(place, 0, SLOTS - 1))
        factor = left_f32[k]
        keep = lax.broadcasted_iota(jnp.int32, factor.shape, 0) < ranks[0, 0, k]
        factor = jnp.where(keep, factor, 0.0)
        upper.append(factor[:half_rank])
        lower.append(factor[half_rank:])
    high, low = parts(jnp.transpose(jnp.concatenate(upper + lower, axis=0)))
    left[:, pl.ds(0, 2 * depth)] = high
    left[:, pl.ds(2 * depth, 2 * depth)] = low

    load_mixing.wait()
    load_index.wait()
    table_len = mixing.shape[2]
    own_index = index[pl.ds(group, 1), :]
    picker = lax.broadcasted_iota(jnp.int32, (table_len, part), 0) == own_index
    picker = jnp.transpose(picker.astype(jnp.float32))
    for a in range(kerns):
        weights = lax.dot_general(
            picker,
            mixing[a],
            (((1,), (1,)), ((), ())),
            precision=lax.Precision.HIGHEST,
            preferred_element_type=jnp.float32,
        )
        for b in range(kerns):
            blend[a, b] = packed(jnp.broadcast_to(weights[:, b : b + 1], (part, cols)))

    for place in range(SLOTS):
        sends[0, 1].append(send_coeffs(0, 1, place))

    def collect(turn, half):
        for place in reversed(range(SLOTS)):
            sends[turn, half][place].wait_recv()
        upper, lower = pairs(jnp.concatenate([arrived[turn][half][place] for place in places], axis=0))
        for at, value in enumerate((upper, lower, upper, lower)):
            arrived_pair[pl.ds(at * depth, depth)] = value
        total[half] += dot(left[...], arrived_pair[...])

    turns = tuple(sorted(range(1, kerns), key=lambda ahead: -min(ahead, kerns - ahead)))
    field_copies = {}

    def send_field(way, half, ahead):
        copy = pltpu.make_async_remote_copy(
            src_ref=mixed_out.at[half, ahead] if way else fields.at[half, ahead],
            dst_ref=second.at[half, group] if way else gathered.at[half, kerns - ahead],
            send_sem=field_send.at[way, half, ahead],
            recv_sem=field_recv.at[way, half, kerns - ahead],
            device_id=(kern_of(ahead), me),
            device_id_type=MESH,
        )
        copy.start()
        field_copies[way, half, ahead] = copy

    def send_first(half):
        for ahead in turns + (0,):
            at = pl.ds(pl.multiple_of(kern_of(ahead) * part, part), part)
            fields[half, ahead] = packed(doubled(total[half, at]))
        for ahead in turns:
            send_field(0, half, ahead)

    def mix(half):
        for ahead in turns:
            field_copies[0, half, ahead].wait_recv()
        for ahead in turns + (0,):
            value = blend[kern_of(ahead), group] * fields[half, 0]
            for other in range(1, kerns):
                value += blend[kern_of(ahead), kern_of(other)] * gathered[half, other]
            if ahead:
                mixed_out[half, ahead] = value
            else:
                second[half, group] = value
        for ahead in turns:
            send_field(1, half, ahead)

    def spread(half, after_second=None):
        for ahead in turns:
            field_copies[1, half, ahead].wait_recv()
        for quarter in range(kerns):
            upper, lower = pairs(second[half, quarter])
            set_pair(quarter * part, half, upper)
            set_pair(quarter * part + part // 2, half, lower)
        for step, (first, end) in enumerate(BLOCKS):
            result = dot(right[pl.ds(first * rank_max, (end - first) * rank_max)], pair[:, lanes(half)])
            keep_coeffs(1, half, first, result)
            for place in range(first, end):
                sends[1, half].append(send_coeffs(1, half, place))
            if step == 1 and after_second is not None:
                after_second()

    collect(0, 0)
    send_first(0)
    mix(0)
    collect(0, 1)
    send_first(1)
    spread(0, lambda: mix(1))
    spread(1)
    diag_part()
    for half in range(HALVES):
        collect(1, half)
    for step in range(kerns):
        at = pl.ds(step * part, part)
        value = doubled(total[0, at])
        out_ref[at] = jnp.where(left_lanes(value), value, doubled(total[1, at]))
    for copies in sends.values():
        for copy in copies:
            copy.wait_send()
    for copy in field_copies.values():
        copy.wait_send()


def local(tiles, kerns, *args):
    diag, left, right, offsets, ranks, mixing, index, rhs = args
    rows, cols = rhs.shape[1:]
    count, rank_max = left.shape[2:4]
    part = rows // kerns
    index = index.reshape(kerns, part)
    mixing = mixing.transpose(1, 2, 0)
    depth = count * rank_max // 2
    operands = (diag, left, right, offsets, ranks, mixing, index, rhs)
    operands = [pltpu.with_memory_space_constraint(value, pltpu.HBM) for value in operands]
    f32, bf16 = jnp.float32, jnp.bfloat16
    vmem = pltpu.VMEM
    return pl.pallas_call(
        functools.partial(kernel, tiles, kerns),
        out_shape=jax.ShapeDtypeStruct((rows, cols), f32),
        in_specs=[pl.BlockSpec(memory_space=pl.ANY)] * 8,
        out_specs=pl.BlockSpec(memory_space=pltpu.VMEM),
        scratch_shapes=[
            vmem((rows, cols), f32),
            vmem((rows, rows), f32),
            vmem((count, rank_max, rows), f32),
            vmem((SLOTS, rank_max, rows), f32),
            pltpu.SMEM(offsets.shape, jnp.int32),
            pltpu.SMEM(ranks.shape, jnp.int32),
            vmem(mixing.shape, f32),
            vmem(index.shape, jnp.int32),
            vmem((rows, 2 * rows), bf16),
            vmem((SLOTS * rank_max, 2 * rows), bf16),
            vmem((rows, 4 * depth), bf16),
            vmem((2 * rows, HALVES * cols), bf16),
            vmem((4 * depth, cols), bf16),
            vmem((2, HALVES, SLOTS, rank_max // 2, cols), f32),
            vmem((SLOTS, rank_max // 2, cols), f32),
            vmem((SLOTS, rank_max // 2, cols), f32),
            vmem((SLOTS, rank_max // 2, cols), f32),
            vmem((SLOTS, rank_max // 2, cols), f32),
            vmem((HALVES, rows, cols), f32),
            vmem((kerns, kerns, part // 2, cols), f32),
            vmem((HALVES, kerns, part // 2, cols), f32),
            vmem((HALVES, kerns, part // 2, cols), f32),
            vmem((HALVES, kerns, part // 2, cols), f32),
            vmem((HALVES, kerns, part // 2, cols), f32),
            pltpu.SemaphoreType.DMA((7,)),
            pltpu.SemaphoreType.DMA((SLOTS,)),
            pltpu.SemaphoreType.DMA((2, HALVES, SLOTS)),
            pltpu.SemaphoreType.DMA((2, HALVES, SLOTS)),
            pltpu.SemaphoreType.DMA((2, HALVES, kerns)),
            pltpu.SemaphoreType.DMA((2, HALVES, kerns)),
        ],
        compiler_params=pltpu.CompilerParams(collective_id=0, has_side_effects=True, vmem_limit_bytes=24 * 2**20),
    )(*operands)[None]


def solution(mesh):
    in_specs = (
        P("kern", "tile", None, None),
        P("kern", "tile", None, None, None),
        P("kern", "tile", None, None, None),
        P("kern", "tile", None),
        P("kern", "tile", None),
        P(),
        P("tile"),
        P("kern", "tile", None),
    )
    out_specs = P("kern", "tile", None)
    step = functools.partial(local, mesh.shape["tile"], mesh.shape["kern"])
    return jax.shard_map(step, mesh=mesh, in_specs=in_specs, out_specs=out_specs, check_vma=False)
```

time: 189 us -> 48.5 us (0.26)
  the two profiles are of different devices: /device:TPU:8 before, /device:TPU:1 now
where the time goes in v2:
time: 48.5 us; the launch traced here: 48.4 us
  Pallas kernels  47.7 us (98%)
  local copies, waits for them, and re-layouts  0.71 us (1%)
    pallas_call x1, Pallas kernels, local(): pl.pallas_call(functools.partial(kernel, tiles, kerns), out_shape=jax.Sha...  47.7 us

profile of v2, /device:TPU:1, one launch (start us, length us, event | category | flops | bytes accessed | tf_op | source)
XLA Modules:
  0.0 48.4 jit_solution(10573087861524133017)
XLA Ops:
  0.0 47.7 %shard_map.82 = f32[512,128]{1,0:T(8,128)S(1)} custom-call(f32[1,1,512,512]{3,2,1,0:T(8,128)} %diag_hbm.1, f32[1,1,8,80,512]{4,3,2,1,0:T(8,128)} %left_hbm.1, f32[1,1,12,80,512]{4,3,2,1,0:T(8,128)} %right_hbm.1, s32[1,1,8]{2,1,0:T(1,128)} %offsets_hbm.1, s32[1,1,8]{2,1,0:T(1,128)} %ranks_hbm.1, f32[4,4,64]{2,1,0:T(4,128)} %bitcast.4, s32[4,128]{1,0:T(4,128)} %bitcast.5, ...), custom_call_target="tpu_custom_call" | custom-call | tf_op jit(solution)/shard_map/pallas_call | solution.py:330
  47.7 0.7 %copy.10 = f32[1,512,128]{2,1,0:T(8,128)} copy(f32[1,512,128]{2,1,0:T(8,128)S(1)} %bitcast.3) | data formatting | bytes 524288

commit v3 on v2

--- a/solution.py
+++ b/solution.py
@@ -116,19 +116,29 @@
     def lanes(half):
         return pl.ds(half * cols, cols)
 
+    load_rhs = pltpu.make_async_copy(rhs_hbm.at[0], column, load_sem.at[0])
+    load_rhs.start()
+
+    def right_block(block):
+        first, end = BLOCKS[block]
+        at = right_f32.at[pl.ds(first, end - first)]
+        return pltpu.make_async_copy(at, at, right_sem.at[block])
+
+    def load_right(block):
+        for place in range(*BLOCKS[block]):
+            source = right_hbm.at[0, 0, ORDER[place]]
+            pltpu.make_async_copy(source, right_f32.at[place], right_sem.at[block]).start()
+
+    load_right(0)
+
     barrier = pltpu.get_barrier_semaphore()
     for slot in ORDER:
         pl.semaphore_signal(barrier, inc=1, device_id=tile_at(offset_of(slot)), device_id_type=MESH)
     for ahead in range(1, kerns):
         pl.semaphore_signal(barrier, inc=1, device_id=(kern_of(ahead), me), device_id_type=MESH)
 
-    load_rhs = pltpu.make_async_copy(rhs_hbm.at[0], column, load_sem.at[0])
-    load_rhs.start()
-    load_right = []
-    for place, slot in enumerate(ORDER):
-        copy = pltpu.make_async_copy(right_hbm.at[0, 0, slot], right_f32.at[place], right_sem.at[place])
-        copy.start()
-        load_right.append(copy)
+    for block in range(1, len(BLOCKS)):
+        load_right(block)
     load_diag = pltpu.make_async_copy(diag_hbm.at[0, 0], diag_f32, load_sem.at[1])
     load_left = pltpu.make_async_copy(left_hbm.at[0, 0], left_f32, load_sem.at[2])
     load_offsets = pltpu.make_async_copy(offsets_hbm, offsets, load_sem.at[3])
@@ -142,13 +152,12 @@
         copy = pltpu.make_async_remote_copy(
             src_ref=coeffs.at[turn, half, place],
             dst_ref=arrived[turn][half].at[place],
-            send_sem=send_sem.at[turn, half, place],
-            recv_sem=recv_sem.at[turn, half, place],
+            send_sem=send_sem,
+            recv_sem=recv_sem.at[turn, half],
             device_id=tile_at(-offset_of(ORDER[place])),
             device_id_type=MESH,
         )
         copy.start()
-        return copy
 
     def set_pair(at, half, value):
         pair[pl.ds(at, value.shape[0]), lanes(half)] = value
@@ -162,10 +171,9 @@
     load_rhs.wait()
     for half, value in enumerate(pairs(column[...])):
         set_pair(0, half, value)
-    sends = {(0, 0): [], (0, 1): [], (1, 0): [], (1, 1): []}
-    for first, end in BLOCKS:
+    for block, (first, end) in enumerate(BLOCKS):
+        right_block(block).wait()
         for place in range(first, end):
-            load_right[place].wait()
             high, low = parts(right_f32[place])
             at = pl.ds(place * rank_max, rank_max)
             right[at, pl.ds(0, rows)] = high
@@ -176,7 +184,7 @@
         if first == 0:
             pl.semaphore_wait(barrier, SLOTS + kerns - 1)
         for place in range(first, end):
-            sends[0, 0].append(send_coeffs(0, 0, place))
+            send_coeffs(0, 0, place)
 
     def diag_part():
         def body(step, carry):
@@ -233,30 +241,32 @@
             blend[a, b] = packed(jnp.broadcast_to(weights[:, b : b + 1], (part, cols)))
 
     for place in range(SLOTS):
-        sends[0, 1].append(send_coeffs(0, 1, place))
+        send_coeffs(0, 1, place)
 
     def collect(turn, half):
-        for place in reversed(range(SLOTS)):
-            sends[turn, half][place].wait_recv()
-        upper, lower = pairs(jnp.concatenate([arrived[turn][half][place] for place in places], axis=0))
+        buffer = arrived[turn][half]
+        pltpu.make_async_copy(buffer, buffer, recv_sem.at[turn, half]).wait()
+        upper, lower = pairs(jnp.concatenate([buffer[place] for place in places], axis=0))
         for at, value in enumerate((upper, lower, upper, lower)):
             arrived_pair[pl.ds(at * depth, depth)] = value
         total[half] += dot(left[...], arrived_pair[...])
 
     turns = tuple(sorted(range(1, kerns), key=lambda ahead: -min(ahead, kerns - ahead)))
-    field_copies = {}
+
+    def wait_fields(way, half):
+        size = gathered.at[half, pl.ds(1, kerns - 1)]
+        pltpu.make_async_copy(size, size, field_recv.at[way, half]).wait()
 
     def send_field(way, half, ahead):
         copy = pltpu.make_async_remote_copy(
             src_ref=mixed_out.at[half, ahead] if way else fields.at[half, ahead],
             dst_ref=second.at[half, group] if way else gathered.at[half, kerns - ahead],
-            send_sem=field_send.at[way, half, ahead],
-            recv_sem=field_recv.at[way, half, kerns - ahead],
+            send_sem=field_send.at[way],
+            recv_sem=field_recv.at[way, half],
             device_id=(kern_of(ahead), me),
             device_id_type=MESH,
         )
         copy.start()
-        field_copies[way, half, ahead] = copy
 
     def send_first(half):
         for ahead in turns + (0,):
@@ -266,8 +276,7 @@
             send_field(0, half, ahead)
 
     def mix(half):
-        for ahead in turns:
-            field_copies[0, half, ahead].wait_recv()
+        wait_fields(0, half)
         for ahead in turns + (0,):
             value = blend[kern_of(ahead), group] * fields[half, 0]
             for other in range(1, kerns):
@@ -280,8 +289,7 @@
             send_field(1, half, ahead)
 
     def spread(half, after_second=None):
-        for ahead in turns:
-            field_copies[1, half, ahead].wait_recv()
+        wait_fields(1, half)
         for quarter in range(kerns):
             upper, lower = pairs(second[half, quarter])
             set_pair(quarter * part, half, upper)
@@ -290,7 +298,7 @@
             result = dot(right[pl.ds(first * rank_max, (end - first) * rank_max)], pair[:, lanes(half)])
             keep_coeffs(1, half, first, result)
             for place in range(first, end):
-                sends[1, half].append(send_coeffs(1, half, place))
+                send_coeffs(1, half, place)
             if step == 1 and after_second is not None:
                 after_second()
 
@@ -308,11 +316,10 @@
         at = pl.ds(step * part, part)
         value = doubled(total[0, at])
         out_ref[at] = jnp.where(left_lanes(value), value, doubled(total[1, at]))
-    for copies in sends.values():
-        for copy in copies:
-            copy.wait_send()
-    for copy in field_copies.values():
-        copy.wait_send()
+    pltpu.make_async_copy(coeffs, coeffs, send_sem).wait()
+    for way, ref in enumerate((fields, mixed_out)):
+        size = ref.at[:, pl.ds(1, kerns - 1)]
+        pltpu.make_async_copy(size, size, field_send.at[way]).wait()
 
 
 def local(tiles, kerns, *args):
@@ -358,11 +365,11 @@
             vmem((HALVES, kerns, part // 2, cols), f32),
             vmem((HALVES, kerns, part // 2, cols), f32),
             pltpu.SemaphoreType.DMA((7,)),
-            pltpu.SemaphoreType.DMA((SLOTS,)),
-            pltpu.SemaphoreType.DMA((2, HALVES, SLOTS)),
-            pltpu.SemaphoreType.DMA((2, HALVES, SLOTS)),
-            pltpu.SemaphoreType.DMA((2, HALVES, kerns)),
-            pltpu.SemaphoreType.DMA((2, HALVES, kerns)),
+            pltpu.SemaphoreType.DMA((len(BLOCKS),)),
+            pltpu.SemaphoreType.DMA,
+            pltpu.SemaphoreType.DMA((2, HALVES)),
+            pltpu.SemaphoreType.DMA((2,)),
+            pltpu.SemaphoreType.DMA((2, HALVES)),
         ],
         compiler_params=pltpu.CompilerParams(collective_id=0, has_side_effects=True, vmem_limit_bytes=24 * 2**20),
     )(*operands)[None]

time: 48.5 us -> 47.2 us (0.973)
  Pallas kernels: 47.7 us -> 46.4 us
    pallas_call x1, Pallas kernels: 47.7 us -> 46.4 us  [local(): pl.pallas_call(functools.partial(kernel, tiles, kerns), out_shape=jax.Sha...]
where the time goes in v3:
time: 47.2 us; the launch traced here: 47.1 us
  Pallas kernels  46.4 us (98%)
  local copies, waits for them, and re-layouts  0.71 us (2%)
    pallas_call x1, Pallas kernels, local(): pl.pallas_call(functools.partial(kernel, tiles, kerns), out_shape=jax.Sha...  46.4 us

profile of v3, /device:TPU:1, one launch (start us, length us, event | category | flops | bytes accessed | tf_op | source)
XLA Modules:
  0.0 47.1 jit_solution(6022080888030082715)
XLA Ops:
  0.0 46.4 %shard_map.82 = f32[512,128]{1,0:T(8,128)S(1)} custom-call(f32[1,1,512,512]{3,2,1,0:T(8,128)} %diag_hbm.1, f32[1,1,8,80,512]{4,3,2,1,0:T(8,128)} %left_hbm.1, f32[1,1,12,80,512]{4,3,2,1,0:T(8,128)} %right_hbm.1, s32[1,1,8]{2,1,0:T(1,128)} %offsets_hbm.1, s32[1,1,8]{2,1,0:T(1,128)} %ranks_hbm.1, f32[4,4,64]{2,1,0:T(4,128)} %bitcast.4, s32[4,128]{1,0:T(4,128)} %bitcast.5, ...), custom_call_target="tpu_custom_call" | custom-call | tf_op jit(solution)/shard_map/pallas_call | solution.py:337
  46.4 0.7 %copy.10 = f32[1,512,128]{2,1,0:T(8,128)} copy(f32[1,512,128]{2,1,0:T(8,128)S(1)} %bitcast.3) | data formatting | bytes 524288

commit v4 on v3

--- a/solution.py
+++ b/solution.py
@@ -13,6 +13,7 @@
 ORDER = tuple(slot for far in range(REACH, 0, -1) for slot in (REACH - far, REACH + far - 1))
 BLOCKS = ((0, 2), (2, 6), (6, 12))
 HALVES = 2
+PIECES = 2
 
 
 def offset_of(slot):
@@ -181,10 +182,12 @@
         result = dot(right[pl.ds(first * rank_max, (end - first) * rank_max)], pair[...])
         for half in range(HALVES):
             keep_coeffs(0, half, first, result[:, half * cols : half * cols + cols])
-        if first == 0:
+        if block == 1:
             pl.semaphore_wait(barrier, SLOTS + kerns - 1)
-        for place in range(first, end):
-            send_coeffs(0, 0, place)
+            first = 0
+        if block:
+            for place in range(first, end):
+                send_coeffs(0, 0, place)
 
     def diag_part():
         def body(step, carry):
@@ -253,16 +256,19 @@
 
     turns = tuple(sorted(range(1, kerns), key=lambda ahead: -min(ahead, kerns - ahead)))
 
-    def wait_fields(way, half):
-        size = gathered.at[half, pl.ds(1, kerns - 1)]
-        pltpu.make_async_copy(size, size, field_recv.at[way, half]).wait()
-
-    def send_field(way, half, ahead):
+    rest = part // 2 // PIECES
+
+    def wait_fields(way, half, piece):
+        size = gathered.at[half, pl.ds(1, kerns - 1), pl.ds(piece * rest, rest)]
+        pltpu.make_async_copy(size, size, field_recv.at[way, half, piece]).wait()
+
+    def send_field(way, half, ahead, piece):
+        at = pl.ds(piece * rest, rest)
         copy = pltpu.make_async_remote_copy(
-            src_ref=mixed_out.at[half, ahead] if way else fields.at[half, ahead],
-            dst_ref=second.at[half, group] if way else gathered.at[half, kerns - ahead],
+            src_ref=mixed_out.at[half, ahead, at] if way else fields.at[half, ahead, at],
+            dst_ref=second.at[half, group, at] if way else gathered.at[half, kerns - ahead, at],
             send_sem=field_send.at[way],
-            recv_sem=field_recv.at[way, half],
+            recv_sem=field_recv.at[way, half, piece],
             device_id=(kern_of(ahead), me),
             device_id_type=MESH,
         )
@@ -272,24 +278,28 @@
         for ahead in turns + (0,):
             at = pl.ds(pl.multiple_of(kern_of(ahead) * part, part), part)
             fields[half, ahead] = packed(doubled(total[half, at]))
-        for ahead in turns:
-            send_field(0, half, ahead)
+        for piece in range(PIECES):
+            for ahead in turns:
+                send_field(0, half, ahead, piece)
 
     def mix(half):
-        wait_fields(0, half)
-        for ahead in turns + (0,):
-            value = blend[kern_of(ahead), group] * fields[half, 0]
-            for other in range(1, kerns):
-                value += blend[kern_of(ahead), kern_of(other)] * gathered[half, other]
-            if ahead:
-                mixed_out[half, ahead] = value
-            else:
-                second[half, group] = value
-        for ahead in turns:
-            send_field(1, half, ahead)
+        for piece in range(PIECES):
+            at = pl.ds(piece * rest, rest)
+            wait_fields(0, half, piece)
+            for ahead in turns + (0,):
+                value = blend[kern_of(ahead), group, at] * fields[half, 0, at]
+                for other in range(1, kerns):
+                    value += blend[kern_of(ahead), kern_of(other), at] * gathered[half, other, at]
+                if ahead:
+                    mixed_out[half, ahead, at] = value
+                else:
+                    second[half, group, at] = value
+            for ahead in turns:
+                send_field(1, half, ahead, piece)
 
     def spread(half, after_second=None):
-        wait_fields(1, half)
+        for piece in range(PIECES):
+            wait_fields(1, half, piece)
         for quarter in range(kerns):
             upper, lower = pairs(second[half, quarter])
             set_pair(quarter * part, half, upper)
@@ -310,11 +320,14 @@
     spread(0, lambda: mix(1))
     spread(1)
     diag_part()
-    for half in range(HALVES):
-        collect(1, half)
+    collect(1, 0)
     for step in range(kerns):
         at = pl.ds(step * part, part)
-        value = doubled(total[0, at])
+        total[0, at] = doubled(total[0, at])
+    collect(1, 1)
+    for step in range(kerns):
+        at = pl.ds(step * part, part)
+        value = total[0, at]
         out_ref[at] = jnp.where(left_lanes(value), value, doubled(total[1, at]))
     pltpu.make_async_copy(coeffs, coeffs, send_sem).wait()
     for way, ref in enumerate((fields, mixed_out)):
@@ -369,7 +382,7 @@
             pltpu.SemaphoreType.DMA,
             pltpu.SemaphoreType.DMA((2, HALVES)),
             pltpu.SemaphoreType.DMA((2,)),
-            pltpu.SemaphoreType.DMA((2, HALVES)),
+            pltpu.SemaphoreType.DMA((2, HALVES, PIECES)),
         ],
         compiler_params=pltpu.CompilerParams(collective_id=0, has_side_effects=True, vmem_limit_bytes=24 * 2**20),
     )(*operands)[None]

time: 47.2 us -> 46.9 us (level)
  no operation moved by 1% of the time
where the time goes in v4:
time: 46.9 us; the launch traced here: 47 us
  Pallas kernels  46.3 us (99%)
  local copies, waits for them, and re-layouts  0.71 us (2%)
    pallas_call x1, Pallas kernels, local(): pl.pallas_call(functools.partial(kernel, tiles, kerns), out_shape=jax.Sha...  46.3 us

profile of v4, /device:TPU:1, one launch (start us, length us, event | category | flops | bytes accessed | tf_op | source)
XLA Modules:
  0.0 47.0 jit_solution(12228275795601206832)
XLA Ops:
  0.0 46.3 %shard_map.82 = f32[512,128]{1,0:T(8,128)S(1)} custom-call(f32[1,1,512,512]{3,2,1,0:T(8,128)} %diag_hbm.1, f32[1,1,8,80,512]{4,3,2,1,0:T(8,128)} %left_hbm.1, f32[1,1,12,80,512]{4,3,2,1,0:T(8,128)} %right_hbm.1, s32[1,1,8]{2,1,0:T(1,128)} %offsets_hbm.1, s32[1,1,8]{2,1,0:T(1,128)} %ranks_hbm.1, f32[4,4,64]{2,1,0:T(4,128)} %bitcast.4, s32[4,128]{1,0:T(4,128)} %bitcast.5, ...), custom_call_target="tpu_custom_call" | custom-call | tf_op jit(solution)/shard_map/pallas_call | solution.py:350
  46.3 0.7 %copy.10 = f32[1,512,128]{2,1,0:T(8,128)} copy(f32[1,512,128]{2,1,0:T(8,128)S(1)} %bitcast.3) | data formatting | bytes 524288

commit v5 on v4

--- a/solution.py
+++ b/solution.py
@@ -246,13 +246,18 @@
     for place in range(SLOTS):
         send_coeffs(0, 1, place)
 
-    def collect(turn, half):
+    def collect(turn, half, finish=None):
         buffer = arrived[turn][half]
         pltpu.make_async_copy(buffer, buffer, recv_sem.at[turn, half]).wait()
         upper, lower = pairs(jnp.concatenate([buffer[place] for place in places], axis=0))
         for at, value in enumerate((upper, lower, upper, lower)):
             arrived_pair[pl.ds(at * depth, depth)] = value
-        total[half] += dot(left[...], arrived_pair[...])
+        if finish is None:
+            total[half] += dot(left[...], arrived_pair[...])
+            return
+        for step in range(2):
+            at = pl.ds(step * rows // 2, rows // 2)
+            finish(at, total[half, at] + dot(left[at], arrived_pair[...]))
 
     turns = tuple(sorted(range(1, kerns), key=lambda ahead: -min(ahead, kerns - ahead)))
 
@@ -324,11 +329,11 @@
     for step in range(kerns):
         at = pl.ds(step * part, part)
         total[0, at] = doubled(total[0, at])
-    collect(1, 1)
-    for step in range(kerns):
-        at = pl.ds(step * part, part)
-        value = total[0, at]
-        out_ref[at] = jnp.where(left_lanes(value), value, doubled(total[1, at]))
+
+    def finish(at, value):
+        out_ref[at] = jnp.where(left_lanes(value), total[0, at], doubled(value))
+
+    collect(1, 1, finish)
     pltpu.make_async_copy(coeffs, coeffs, send_sem).wait()
     for way, ref in enumerate((fields, mixed_out)):
         size = ref.at[:, pl.ds(1, kerns - 1)]

time: 46.9 us -> 47.1 us (level)
  no operation moved by 1% of the time
where the time goes in v5:
time: 47.1 us; the launch traced here: 47 us
  Pallas kernels  46.3 us (98%)
  local copies, waits for them, and re-layouts  0.71 us (2%)
    pallas_call x1, Pallas kernels, local(): pl.pallas_call(functools.partial(kernel, tiles, kerns), out_shape=jax.Sha...  46.3 us

profile of v5, /device:TPU:1, one launch (start us, length us, event | category | flops | bytes accessed | tf_op | source)
XLA Modules:
  0.0 47.0 jit_solution(10594198740651065719)
XLA Ops:
  0.0 46.3 %shard_map.82 = f32[512,128]{1,0:T(8,128)S(1)} custom-call(f32[1,1,512,512]{3,2,1,0:T(8,128)} %diag_hbm.1, f32[1,1,8,80,512]{4,3,2,1,0:T(8,128)} %left_hbm.1, f32[1,1,12,80,512]{4,3,2,1,0:T(8,128)} %right_hbm.1, s32[1,1,8]{2,1,0:T(1,128)} %offsets_hbm.1, s32[1,1,8]{2,1,0:T(1,128)} %ranks_hbm.1, f32[4,4,64]{2,1,0:T(4,128)} %bitcast.4, s32[4,128]{1,0:T(4,128)} %bitcast.5, ...), custom_call_target="tpu_custom_call" | custom-call | tf_op jit(solution)/shard_map/pallas_call | solution.py:355
  46.3 0.7 %copy.10 = f32[1,512,128]{2,1,0:T(8,128)} copy(f32[1,512,128]{2,1,0:T(8,128)S(1)} %bitcast.3) | data formatting | bytes 524288
